TPU v7x, 512 devices: a whole 4x8x8 slice. The times are simulated.
512 devices in a mesh: view: 8 (over z_hi, x), col: 64 (over y, z_lo, core).
Axes of the slice: x: 4, y: 8, z: 8 (z_hi: 2, z_lo: 4; z = z_hi * 4 + z_lo), core: 2. Of those that a mesh axis runs over, the one named last changes fastest.
Arguments:
- estimate: float32 [2048, 64, 128], P('col', 'view'), may hold values from 0.5 to 2
- observed: float32 [8, 2048, 64, 128], P('view', 'col'), may hold values from 0.5 to 2
- psf_taps: float32 [8, 3, 31], replicated, as said below
- intersection: int32 [8, 16], replicated, may hold values 0 or 1
Outputs:
- deconvolved: float32 [2048, 64, 128], P('col', 'view')
Inputs may be any that keep to these rules, and one draw needn't show every extreme that they name: `psf_taps`: every tap is positive.
All inputs are finite; a program needn't handle non-finite values.
Results may differ from a plain program's by a relative error of at most 0.0003.
Values sent between devices are 32-bit elements; how exact they have to be, the bound alone decides.
No kernel may reach another device: no remote copies, remote signals or barrier semaphores. Data moves between devices by JAX's collectives and lax.ppermute only.
A program may use at most 64 MiB of HBM per device.

v0:
```python
from functools import partial
import jax
import jax.numpy as jnp
from jax import lax
from jax.sharding import PartitionSpec as P

TX = 128
ITERS = 2
HIGH = lax.Precision.HIGHEST


def extended_2(block, sides, width):
    for axis, dim in sides:
        count = lax.axis_size(axis)
        forward = [(i, i + 1) for i in range(count - 1)]
        backward = [(target, source) for source, target in forward]
        low = lax.ppermute(
            lax.slice_in_dim(block, block.shape[dim] - width, None, axis=dim), axis, forward
        )
        high = lax.ppermute(lax.slice_in_dim(block, 0, width, axis=dim), axis, backward)
        block = jnp.concatenate([low, block, high], axis=dim)
    return block


def banded(kernel, length):
    tap_count = kernel.shape[0]
    half_width = (tap_count - 1) // 2
    offsets = jnp.arange(length)[:, None] - jnp.arange(length)[None, :] + half_width
    onehot = (offsets[:, :, None] == jnp.arange(tap_count)[None, None, :]).astype(jnp.float32)
    return jnp.einsum("iok,k->io", onehot, kernel, precision=HIGH)


def column_weights(kernel, length):
    return jnp.sum(banded(kernel, length), axis=0)


def row_matrix(kernel, row_count, row_span):
    tap_count = kernel.shape[-1]
    offsets = jnp.arange(row_span)[None, :] - jnp.arange(row_count)[:, None]
    onehot = (offsets[:, :, None] == jnp.arange(tap_count)[None, None, :]).astype(jnp.float32)
    return jnp.einsum("xjk,k->xj", onehot, kernel, precision=HIGH)


def along_rows(extended, kernel):
    row_span = extended.shape[0]
    row_count = row_span - (kernel.shape[0] - 1)
    matrix = row_matrix(kernel, row_count, row_span)
    flattened = extended.reshape(row_span, -1)
    result = jnp.dot(matrix, flattened, precision=HIGH)
    return result.reshape((row_count,) + extended.shape[1:])


def across(field, kernels):
    result = jnp.einsum("xyz,yw->xwz", field, banded(kernels[1], field.shape[1]), precision=HIGH)
    return jnp.dot(result, banded(kernels[2], field.shape[2]), precision=HIGH)


def view_masks(intersection, first_row, row_count, tile_rows):
    global_rows = first_row + jnp.arange(row_count, dtype=jnp.int32)
    tile_index = jnp.floor_divide(global_rows, tile_rows)
    onehot = (
        tile_index[:, None] == jnp.arange(intersection.shape[1], dtype=jnp.int32)[None, :]
    ).astype(jnp.float32)
    return jnp.dot(intersection.astype(jnp.float32), onehot.T, precision=HIGH)


def body(estimate, observed, psf_taps, intersection):
    slab_rows = observed.shape[1]
    full_width = observed.shape[2]
    depth = observed.shape[3]
    own_width = estimate.shape[1]
    view_index = lax.axis_index("view")
    col_index = lax.axis_index("col")
    first_row = col_index * slab_rows
    kernels = psf_taps / jnp.sum(psf_taps, axis=2, keepdims=True)
    mirrored = kernels[:, :, ::-1]
    halo_rows = (kernels.shape[2] - 1) // 2
    picker = (jnp.arange(kernels.shape[0], dtype=jnp.int32) == view_index).astype(jnp.float32)
    own_kernels = jnp.einsum("v,vdk->dk", picker, kernels, precision=HIGH)
    own_mirror = own_kernels[:, ::-1]
    masks_all = view_masks(intersection, first_row - halo_rows, slab_rows + 2 * halo_rows, TX)
    row_mats = jax.vmap(
        partial(row_matrix, row_count=slab_rows, row_span=slab_rows + 2 * halo_rows)
    )(mirrored[:, 0])
    weight_rows = jnp.einsum("vxj,vj->vx", row_mats, masks_all, precision=HIGH)
    weight_cols = jax.vmap(partial(column_weights, length=full_width))(mirrored[:, 1])
    weight_depth = jax.vmap(partial(column_weights, length=depth))(mirrored[:, 2])
    weight_full = jnp.einsum(
        "vx,vy,vz->xyz", weight_rows, weight_cols, weight_depth, precision=HIGH
    )
    weight_own = lax.dynamic_slice_in_dim(weight_full, view_index * own_width, own_width, 1)
    mask_outer = jnp.dot(picker, masks_all, precision=HIGH)
    mask_inner = mask_outer[halo_rows : halo_rows + slab_rows]
    image_used = observed[0]
    current = estimate
    for iteration in range(ITERS):
        full_estimate = lax.all_gather(current, "view", axis=1, tiled=True)
        extended = extended_2(full_estimate, (("col", 0),), halo_rows)
        blurred = across(along_rows(extended, own_kernels[0]), own_kernels)
        inside = mask_inner[:, None, None] > 0
        ratio = jnp.where(inside, image_used / jnp.where(inside, blurred, 1.0), 0.0)
        padded_ratio = extended_2(ratio, (("col", 0),), halo_rows)
        summed = lax.psum_scatter(
            across(along_rows(padded_ratio, own_mirror[0]), own_mirror),
            "view",
            scatter_dimension=1,
            tiled=True,
        )
        current = current * (summed + 1.0) / (weight_own + 1.0)
    return current


def solution(mesh):
    return jax.shard_map(
        body,
        mesh=mesh,
        in_specs=(P("col", "view", None), P("view", "col", None, None), P(), P()),
        out_specs=P("col", "view", None),
        check_vma=False,
    )
```

profile of v0, /device:TPU:8, one launch (start us, length us, event | category | flops | bytes accessed | tf_op | source)
XLA Modules:
  0.0 433.1 jit_solution(17454508880146930062)
XLA Ops:
  6.5 0.7 all-gather.3.cloned.1.call-update
  7.3 0.8 reduce_sum.27
  8.1 0.8 broadcast_divide_fusion
  9.0 0.9 fusion.34
  9.9 0.1 convolution_bitcast_fusion.4
  10.2 0.3 fusion.27
  10.5 0.1 iota_compare_fusion.1
  10.6 0.5 fusion.21
  11.2 71.4 %all-gather.3.cloned.1.call-done = f32[32,64,128]{2,1,0:T(8,128)} async-done(((f32[32,8,128]{2,1,0:T(8,128)}), f32[32,64,128]{2,1,0:T(8,128)}) %all-gather.3.cloned.1.call-update) | async-done | bytes 1048592 | tf_op jit(solution)/shard_map/all_gather | solution.py:97
  82.6 1.3 fusion.64
  83.9 1.9 collective-permute-start
  85.9 6.3 %collective-permute-start.1 = (f32[15,64,128]{2,1,0:T(8,128)S(1)}, f32[15,64,128]{2,1,0:T(8,128)}, u32[]{:S(2)}, u32[]{:S(2)}) collective-permute-start(f32[15,64,128]{2,1,0:T(8,128)S(1)} %get-tuple-element.12), channel_id=1, source_target_pairs={{1,0},{2,1},{3,2},{4,3},{5,4},{6,5},{7,6},{8,7},{9,8},{10,9},{11,1... | collective-permute-start | bytes 1474568 | tf_op jit(solution)/shard_map/ppermute | solution.py:20
  92.3 0.3 iota_compare_fusion
  92.6 1.2 fusion.14
  93.8 3.2 collective-permute-done
  97.0 1.5 collective-permute-done.1
  98.6 1.2 pad_maximum_fusion
  99.7 0.2 slice_bitcast_fusion.3
  100.0 2.3 fusion.6
  102.3 1.6 convolution_bitcast_fusion.3
  103.9 1.0 fusion.9
  105.0 5.3 %collective-permute-start.2 = (f32[15,64,128]{2,1,0:T(8,128)S(1)}, f32[15,64,128]{2,1,0:T(8,128)S(1)}, u32[]{:S(2)}, u32[]{:S(2)}) collective-permute-start(f32[15,64,128]{2,1,0:T(8,128)S(1)} %get-tuple-element.9), channel_id=1, source_target_pairs={{0,1},{1,2},{2,3},{3,4},{4,5},{5,6},{6,7},{7,8},{8,9},{9,10},{10,1... | collective-permute-start | bytes 1474568 | tf_op jit(solution)/shard_map/ppermute | solution.py:17
  110.3 3.4 collective-permute-start.3
  113.7 0.3 fusion.28
  114.2 0.5 fusion.23
  114.8 1.2 fusion.12
  116.0 2.4 collective-permute-done.2
  118.3 1.5 collective-permute-done.3
  119.9 1.2 pad_maximum_fusion.1
  121.0 0.2 slice_bitcast_fusion.2
  121.3 2.3 fusion.4
  123.6 1.6 convolution_bitcast_fusion.2
  125.2 2.0 fusion.67
  127.5 0.6 convolution_reduce_fusion.1
  128.2 0.3 fusion.26
  128.4 0.3 fusion.32
  128.8 0.1 broadcast_multiply_fusion
  128.9 0.2 copy.38
  129.1 1.2 convolution_reduce_fusion
  130.2 1.8 fusion.36
  132.1 89.4 %reduce-scatter.3.cloned.1.call-done = f32[32,8,128]{2,1,0:T(8,128)} async-done(((f32[32,64,128]{2,1,0:T(8,128)}), f32[32,8,128]{2,1,0:T(8,128)}) %reduce-scatter.3.cloned.1.call-update) | async-done | bytes 131088 | tf_op jit(solution)/shard_map/reduce_scatter | solution.py:103
  221.4 1.6 bitcast_divide_fusion.1
  223.1 65.0 %all-gather.5.cloned.1.call-done = f32[32,64,128]{2,1,0:T(8,128)} async-done(((f32[32,8,128]{2,1,0:T(8,128)}), f32[32,64,128]{2,1,0:T(8,128)}) %all-gather.5.cloned.1.call-update) | async-done | bytes 1048592 | tf_op jit(solution)/shard_map/all_gather | solution.py:97
  288.1 1.4 fusion.62
  289.4 1.9 collective-permute-start.4
  291.4 6.6 %collective-permute-start.5 = (f32[15,64,128]{2,1,0:T(8,128)S(1)}, f32[15,64,128]{2,1,0:T(8,128)S(1)}, u32[]{:S(2)}, u32[]{:S(2)}) collective-permute-start(f32[15,64,128]{2,1,0:T(8,128)S(1)} %get-tuple-element.8), channel_id=1, source_target_pairs={{1,0},{2,1},{3,2},{4,3},{5,4},{6,5},{7,6},{8,7},{9,8},{10,9},{11,1... | collective-permute-start | bytes 1474568 | tf_op jit(solution)/shard_map/ppermute | solution.py:20
  297.9 4.6 %collective-permute-done.4 = f32[15,64,128]{2,1,0:T(8,128)S(1)} collective-permute-done((f32[15,64,128]{2,1,0:T(8,128)S(1)}, f32[15,64,128]{2,1,0:T(8,128)S(1)}, u32[]{:S(2)}, u32[]{:S(2)}) %collective-permute-start.4) | collective-permute-done | bytes 491552 | tf_op jit(solution)/shard_map/ppermute | solution.py:17
  302.5 1.5 collective-permute-done.5
  304.0 0.2 pad_maximum_fusion.2
  304.3 0.2 slice_bitcast_fusion.1
  304.5 2.3 fusion.2
  306.8 1.6 convolution_bitcast_fusion.1
  308.5 1.0 fusion.11
  309.6 5.2 %collective-permute-start.6 = (f32[15,64,128]{2,1,0:T(8,128)S(1)}, f32[15,64,128]{2,1,0:T(8,128)S(1)}, u32[]{:S(2)}, u32[]{:S(2)}) collective-permute-start(f32[15,64,128]{2,1,0:T(8,128)S(1)} %get-tuple-element.5), channel_id=1, source_target_pairs={{0,1},{1,2},{2,3},{3,4},{4,5},{5,6},{6,7},{7,8},{8,9},{9,10},{10,1... | collective-permute-start | bytes 1474568 | tf_op jit(solution)/shard_map/ppermute | solution.py:17
  314.7 3.3 collective-permute-start.7
  318.0 4.8 %collective-permute-done.6 = f32[15,64,128]{2,1,0:T(8,128)S(1)} collective-permute-done((f32[15,64,128]{2,1,0:T(8,128)S(1)}, f32[15,64,128]{2,1,0:T(8,128)S(1)}, u32[]{:S(2)}, u32[]{:S(2)}) %collective-permute-start.6) | collective-permute-done | bytes 491552 | tf_op jit(solution)/shard_map/ppermute | solution.py:17
  322.8 1.5 collective-permute-done.7
  324.3 0.2 pad_maximum_fusion.3
  324.6 0.2 slice_bitcast_fusion
  324.8 2.3 fusion
  327.1 1.6 convolution_bitcast_fusion
  328.8 2.0 fusion.68
  330.7 94.2 %reduce-scatter.5.cloned.1.call-done = f32[32,8,128]{2,1,0:T(8,128)} async-done(((f32[32,64,128]{2,1,0:T(8,128)}), f32[32,8,128]{2,1,0:T(8,128)}) %reduce-scatter.5.cloned.1.call-update) | async-done | bytes 131088 | tf_op jit(solution)/shard_map/reduce_scatter | solution.py:103
  424.9 1.6 bitcast_divide_fusion
  (49 shorter events, 1.2 us)
Async XLA Ops:
  6.5 76.1 %all-gather.3.cloned.1.call-start = ((), (), s32[]{:S(2)}) async-start(), calls=%async_computation.2 | async-start | bytes 1179648 | tf_op jit(solution)/shard_map/all_gather | solution.py:97
  7.3 214.2 %reduce-scatter.3.cloned.1.call-start = ((), (), s32[]{:S(2)}) async-start(), calls=%async_computation.3 | async-start | bytes 1179648 | tf_op jit(solution)/shard_map/reduce_scatter | solution.py:103
  10.6 103.6 %copy-start.4 = (pred[64,64,31]{1,0,2:T(32,128)(4,1)}, pred[64,64,31]{1,0,2:T(32,128)(4,1)S(1)}, u32[]{:S(2)}) copy-start(pred[64,64,31]{1,0,2:T(32,128)(4,1)S(1)} %iota_compare_fusion.1) | copy-start | bytes 380932
  11.2 91.1 %copy-start.6 = (f32[1,64,64]{2,0,1:T(1,128)}, f32[1,64,64]{2,0,1:T(1,128)S(1)}, u32[]{:S(2)}) copy-start(f32[1,64,64]{2,0,1:T(1,128)S(1)} %fusion.21) | copy-start | bytes 49156
  82.6 15.9 %copy-start = (f32[32,64,128]{2,1,0:T(8,128)S(1)}, f32[32,64,128]{2,1,0:T(8,128)}, u32[]{:S(2)}) copy-start(f32[32,64,128]{2,1,0:T(8,128)} %all-gather.3.cloned.1.call-done) | copy-start | bytes 3145732
  83.9 13.1 %collective-permute-start = (f32[15,64,128]{2,1,0:T(8,128)S(1)}, f32[15,64,128]{2,1,0:T(8,128)S(1)}, u32[]{:S(2)}, u32[]{:S(2)}) collective-permute-start(f32[15,64,128]{2,1,0:T(8,128)S(1)} %get-tuple-element.11), channel_id=1, source_target_pairs={{0,1},{1,2},{2,3},{3,4},{4,5},{5,6},{6,7},{7,8},{8,9},{9,10},{10,1... | collective-permute-start | bytes 1474568 | tf_op jit(solution)/shard_map/ppermute | solution.py:17
  85.9 12.7 %collective-permute-start.1 = (f32[15,64,128]{2,1,0:T(8,128)S(1)}, f32[15,64,128]{2,1,0:T(8,128)}, u32[]{:S(2)}, u32[]{:S(2)}) collective-permute-start(f32[15,64,128]{2,1,0:T(8,128)S(1)} %get-tuple-element.12), channel_id=1, source_target_pairs={{1,0},{2,1},{3,2},{4,3},{5,4},{6,5},{7,6},{8,7},{9,8},{10,9},{11,1... | collective-permute-start | bytes 1474568 | tf_op jit(solution)/shard_map/ppermute | solution.py:20
  100.0 3.9 copy-start.10
  105.0 13.3 %collective-permute-start.2 = (f32[15,64,128]{2,1,0:T(8,128)S(1)}, f32[15,64,128]{2,1,0:T(8,128)S(1)}, u32[]{:S(2)}, u32[]{:S(2)}) collective-permute-start(f32[15,64,128]{2,1,0:T(8,128)S(1)} %get-tuple-element.9), channel_id=1, source_target_pairs={{0,1},{1,2},{2,3},{3,4},{4,5},{5,6},{6,7},{7,8},{8,9},{9,10},{10,1... | collective-permute-start | bytes 1474568 | tf_op jit(solution)/shard_map/ppermute | solution.py:17
  110.3 9.6 %collective-permute-start.3 = (f32[15,64,128]{2,1,0:T(8,128)S(1)}, f32[15,64,128]{2,1,0:T(8,128)}, u32[]{:S(2)}, u32[]{:S(2)}) collective-permute-start(f32[15,64,128]{2,1,0:T(8,128)S(1)} %get-tuple-element.10), channel_id=1, source_target_pairs={{1,0},{2,1},{3,2},{4,3},{5,4},{6,5},{7,6},{8,7},{9,8},{10,9},{11,1... | collective-permute-start | bytes 1474568 | tf_op jit(solution)/shard_map/ppermute | solution.py:20
  114.8 8.8 %copy-start.8 = (f32[1,64,64]{2,0,1:T(1,128)}, f32[1,64,64]{2,0,1:T(1,128)S(1)}, u32[]{:S(2)}) copy-start(f32[1,64,64]{2,0,1:T(1,128)S(1)} %fusion.23) | copy-start | bytes 49156
  125.2 2.3 copy-start.5
  127.2 160.9 %all-gather.5.cloned.1.call-start = ((), (), s32[]{:S(2)}) async-start(), calls=%async_computation.4 | async-start | bytes 1179648 | tf_op jit(solution)/shard_map/all_gather | solution.py:97
  128.1 93.4 %copy-start.3 = (f32[32,8,128]{2,1,0:T(8,128)S(1)}, f32[32,8,128]{2,1,0:T(8,128)}, u32[]{:S(2)}) copy-start(f32[32,8,128]{2,1,0:T(8,128)} %param.4) | copy-start | bytes 393220
  223.1 201.9 %reduce-scatter.5.cloned.1.call-start = ((), (), s32[]{:S(2)}) async-start(), calls=%async_computation.5 | async-start | bytes 1179648 | tf_op jit(solution)/shard_map/reduce_scatter | solution.py:103
  288.1 16.0 %copy-start.1 = (f32[32,64,128]{2,1,0:T(8,128)S(1)}, f32[32,64,128]{2,1,0:T(8,128)}, u32[]{:S(2)}) copy-start(f32[32,64,128]{2,1,0:T(8,128)} %all-gather.5.cloned.1.call-done) | copy-start | bytes 3145732
  289.4 13.1 %collective-permute-start.4 = (f32[15,64,128]{2,1,0:T(8,128)S(1)}, f32[15,64,128]{2,1,0:T(8,128)S(1)}, u32[]{:S(2)}, u32[]{:S(2)}) collective-permute-start(f32[15,64,128]{2,1,0:T(8,128)S(1)} %get-tuple-element.7), channel_id=1, source_target_pairs={{0,1},{1,2},{2,3},{3,4},{4,5},{5,6},{6,7},{7,8},{8,9},{9,10},{10,1... | collective-permute-start | bytes 1474568 | tf_op jit(solution)/shard_map/ppermute | solution.py:17
  291.4 12.7 %collective-permute-start.5 = (f32[15,64,128]{2,1,0:T(8,128)S(1)}, f32[15,64,128]{2,1,0:T(8,128)S(1)}, u32[]{:S(2)}, u32[]{:S(2)}) collective-permute-start(f32[15,64,128]{2,1,0:T(8,128)S(1)} %get-tuple-element.8), channel_id=1, source_target_pairs={{1,0},{2,1},{3,2},{4,3},{5,4},{6,5},{7,6},{8,7},{9,8},{10,9},{11,1... | collective-permute-start | bytes 1474568 | tf_op jit(solution)/shard_map/ppermute | solution.py:20
  304.5 2.3 copy-start.7
  304.5 3.9 copy-start.11
  309.6 13.2 %collective-permute-start.6 = (f32[15,64,128]{2,1,0:T(8,128)S(1)}, f32[15,64,128]{2,1,0:T(8,128)S(1)}, u32[]{:S(2)}, u32[]{:S(2)}) collective-permute-start(f32[15,64,128]{2,1,0:T(8,128)S(1)} %get-tuple-element.5), channel_id=1, source_target_pairs={{0,1},{1,2},{2,3},{3,4},{4,5},{5,6},{6,7},{7,8},{8,9},{9,10},{10,1... | collective-permute-start | bytes 1474568 | tf_op jit(solution)/shard_map/ppermute | solution.py:17
  314.7 9.6 %collective-permute-start.7 = (f32[15,64,128]{2,1,0:T(8,128)S(1)}, f32[15,64,128]{2,1,0:T(8,128)S(1)}, u32[]{:S(2)}, u32[]{:S(2)}) collective-permute-start(f32[15,64,128]{2,1,0:T(8,128)S(1)} %get-tuple-element.6), channel_id=1, source_target_pairs={{1,0},{2,1},{3,2},{4,3},{5,4},{6,5},{7,6},{8,7},{9,8},{10,9},{11,1... | collective-permute-start | bytes 1474568 | tf_op jit(solution)/shard_map/ppermute | solution.py:20
  324.8 2.3 copy-start.9
  328.7 96.2 %copy-start.2 = (f32[32,8,128]{2,1,0:T(8,128)S(1)}, f32[32,8,128]{2,1,0:T(8,128)}, u32[]{:S(2)}) copy-start(f32[32,8,128]{2,1,0:T(8,128)} %bitcast_divide_fusion.1) | copy-start | bytes 393220
Sparse Core Ops, SparseCore 0:
  10.4 72.1 all-gather.2
  127.3 94.0 reduce-scatter.2
  225.0 63.0 all-gather.4
  330.9 94.0 reduce-scatter.4
where the time goes:
time: 434 us; the launch traced here: 433 us
  waiting for transfers between devices  342 us (79%)
  starting transfers between devices  34 us (8%)
  matrix products  30.9 us (7%)
  between operations  13.6 us (3%)
  other arithmetic  8.23 us (2%)
  local copies, waits for them, and re-layouts  4.58 us (1%)
    reduce_scatter x2, waiting for transfers between devices, body(): lax.psum_scatter(across(along_rows(padded_ratio, own_mirror[0]), own_mirr...  184 us
    all_gather x2, waiting for transfers between devices, body(): full_estimate = lax.all_gather(current, 'view', axis=1, tiled=True)  136 us
    ppermute x4, starting transfers between devices, extended_2(): lax.ppermute(lax.slice_in_dim(block, 0, width, axis=dim), axis, backward)  19.6 us
    ppermute x4, waiting for transfers between devices, extended_2(): lax.ppermute(lax.slice_in_dim(block, block.shape[dim] - width, None, axis...  14.9 us
    ppermute x4, starting transfers between devices, extended_2(): lax.ppermute(lax.slice_in_dim(block, block.shape[dim] - width, None, axis...  14.3 us
    dot_general x4, matrix products, along_rows(): result = jnp.dot(matrix, flattened, precision=HIGH)  9.19 us
  transfers between devices with their start and end apart: 12, of which 12 were waited for; matrix products, arithmetic and copies ran while one was open for 3% of the time, Pallas kernels for 0%

commit v1 on v0

--- a/solution.py
+++ b/solution.py
@@ -94,7 +94,9 @@
     image_used = observed[0]
     current = estimate
     for iteration in range(ITERS):
-        full_estimate = lax.all_gather(current, "view", axis=1, tiled=True)
+        full_estimate = jnp.concatenate(
+            lax.all_to_all(jnp.stack([current] * lax.axis_size("view")), "view", 0, 0), axis=1
+        )
         extended = extended_2(full_estimate, (("col", 0),), halo_rows)
         blurred = across(along_rows(extended, own_kernels[0]), own_kernels)
         inside = mask_inner[:, None, None] > 0

time: 434 us -> 362 us (0.83)
  waiting for transfers between devices: 342 us -> 231 us
  blocking collectives: 0 us -> 30 us
  starting transfers between devices: 34 us -> 47 us
  other arithmetic: 8.23 us -> 3.69 us
    all_gather x2 -> x0, waiting for transfers between devices: 136 us -> none  [body(): full_estimate = lax.all_gather(current, 'view', axis=1, tiled=True)]
    all_to_all x0 -> x1, blocking collectives: none -> 30 us  [body(): lax.all_to_all(jnp.stack([current] * lax.axis_size('view')), 'view', 0, 0)]
    all_to_all x0 -> x1, waiting for transfers between devices: none -> 27.6 us  [body(): lax.all_to_all(jnp.stack([current] * lax.axis_size('view')), 'view', 0, 0)]
    all_to_all x0 -> x1, starting transfers between devices: none -> 12.7 us  [body(): lax.all_to_all(jnp.stack([current] * lax.axis_size('view')), 'view', 0, 0)]
  transfers between devices with their start and end apart: 12 -> 11, of which waited for: 12 -> 11; matrix products, arithmetic and copies ran while one was open for 3% -> 3% of each run, Pallas kernels for 0% -> 0%
where the time goes in v1:
time: 362 us
  waiting for transfers between devices  231 us (64%)
  starting transfers between devices  47 us (13%)
  blocking collectives  30 us (8%)
  matrix products  28.9 us (8%)
  between operations  13.9 us (4%)
  local copies, waits for them, and re-layouts  7.69 us (2%)
  other arithmetic  3.69 us (1%)
    reduce_scatter x2, waiting for transfers between devices, body(): lax.psum_scatter(across(along_rows(padded_ratio, own_mirror[0]), own_mirr...  184 us
    all_to_all x1, blocking collectives, body(): lax.all_to_all(jnp.stack([current] * lax.axis_size('view')), 'view', 0, 0)  30 us
    all_to_all x1, waiting for transfers between devices, body(): lax.all_to_all(jnp.stack([current] * lax.axis_size('view')), 'view', 0, 0)  27.6 us
    ppermute x4, starting transfers between devices, extended_2(): lax.ppermute(lax.slice_in_dim(block, 0, width, axis=dim), axis, backward)  19.3 us
    ppermute x4, starting transfers between devices, extended_2(): lax.ppermute(lax.slice_in_dim(block, block.shape[dim] - width, None, axis...  14.9 us
    ppermute x4, waiting for transfers between devices, extended_2(): lax.ppermute(lax.slice_in_dim(block, block.shape[dim] - width, None, axis...  13.7 us
    all_to_all x1, starting transfers between devices, body(): lax.all_to_all(jnp.stack([current] * lax.axis_size('view')), 'view', 0, 0)  12.7 us
    dot_general x4, matrix products, along_rows(): result = jnp.dot(matrix, flattened, precision=HIGH)  9.19 us
  transfers between devices with their start and end apart: 11, of which 11 were waited for; matrix products, arithmetic and copies ran while one was open for 3% of the time, Pallas kernels for 0%

profile of v1, /device:TPU:8, one launch (start us, length us, event | category | flops | bytes accessed | tf_op | source)
XLA Modules:
  0.0 361.9 jit_solution(15189771167026223360)
XLA Ops:
  6.5 2.0 stack.4
  8.5 12.7 %all-to-all-start = ((f32[8,32,8,128]{3,2,1,0:T(8,128)}), f32[8,32,8,128]{3,2,1,0:T(8,128)S(1)}, u32[]{:S(2)}, u32[]{:S(2)}) async-start(f32[8,32,8,128]{3,2,1,0:T(8,128)} %stack.4), calls=%async_computation | async-start | bytes 2097152 | tf_op jit(solution)/shard_map/all_to_all | solution.py:98
  21.6 0.2 fusion.36
  22.1 0.3 fusion.26
  22.4 27.6 %all-to-all-done = f32[8,32,8,128]{3,2,1,0:T(8,128)S(1)} async-done(((f32[8,32,8,128]{3,2,1,0:T(8,128)}), f32[8,32,8,128]{3,2,1,0:T(8,128)S(1)}, u32[]{:S(2)}, u32[]{:S(2)}) %all-to-all-start) | async-done | bytes 1048608 | tf_op jit(solution)/shard_map/all_to_all | solution.py:98
  50.2 1.9 collective-permute-start
  52.1 6.3 %collective-permute-start.1 = (f32[15,64,128]{2,1,0:T(8,128)S(1)}, f32[15,64,128]{2,1,0:T(8,128)S(1)}, u32[]{:S(2)}, u32[]{:S(2)}) collective-permute-start(f32[15,64,128]{2,1,0:T(8,128)S(1)} %get-tuple-element.14), channel_id=1, source_target_pairs={{1,0},{2,1},{3,2},{4,3},{5,4},{6,5},{7,6},{8,7},{9,8},{10,9},{11,1... | collective-permute-start | bytes 1474568 | tf_op jit(solution)/shard_map/ppermute | solution.py:20
  58.6 0.5 fusion.23
  59.1 0.8 fusion.10
  59.9 0.6 copy.87
  60.5 2.7 collective-permute-done
  63.3 0.3 copy.49
  63.6 1.2 collective-permute-done.1
  64.9 0.3 copy.51
  65.2 0.2 pad_maximum_fusion
  65.4 0.4 copy.52
  65.8 0.2 slice_bitcast_fusion.3
  66.0 2.3 fusion.6
  68.3 1.6 convolution_bitcast_fusion.3
  69.9 1.0 fusion.12
  71.0 5.2 %collective-permute-start.2 = (f32[15,64,128]{2,1,0:T(8,128)S(1)}, f32[15,64,128]{2,1,0:T(8,128)S(1)}, u32[]{:S(2)}, u32[]{:S(2)}) collective-permute-start(f32[15,64,128]{2,1,0:T(8,128)S(1)} %get-tuple-element.11), channel_id=1, source_target_pairs={{0,1},{1,2},{2,3},{3,4},{4,5},{5,6},{6,7},{7,8},{8,9},{9,10},{10,1... | collective-permute-start | bytes 1474568 | tf_op jit(solution)/shard_map/ppermute | solution.py:17
  76.3 3.4 collective-permute-start.3
  79.7 0.3 fusion.27
  80.1 0.5 fusion.24
  80.6 0.8 fusion.9
  81.5 2.8 collective-permute-done.2
  84.2 1.6 collective-permute-done.3
  85.9 0.2 slice_bitcast_fusion.2
  86.2 2.3 fusion.4
  88.5 1.6 convolution_bitcast_fusion.2
  90.1 1.9 fusion.69
  92.3 0.5 convolution_reduce_fusion
  92.9 0.3 fusion.25
  93.2 0.3 fusion.34
  93.6 0.2 copy.47
  93.8 0.8 fusion.15
  94.7 1.8 fusion.38
  96.5 90.6 %reduce-scatter.3.cloned.1.call-done = f32[32,8,128]{2,1,0:T(8,128)} async-done(((f32[32,64,128]{2,1,0:T(8,128)}), f32[32,8,128]{2,1,0:T(8,128)}) %reduce-scatter.3.cloned.1.call-update) | async-done | bytes 131088 | tf_op jit(solution)/shard_map/reduce_scatter | solution.py:105
  187.1 0.9 bitcast_divide_fusion.1
  188.1 30.0 %all_to_all.10 = f32[8,32,8,128]{3,2,1,0:T(8,128)S(1)} all-to-all(f32[8,32,8,128]{3,2,1,0:T(8,128)S(1)} %stack.5), channel_id=1, replica_groups=mesh['view'=8,'col'=64] {'view'}, dimensions={0} | all-to-all | bytes 2097152 | tf_op jit(solution)/shard_map/all_to_all | solution.py:98
  218.4 1.9 collective-permute-start.4
  220.3 6.6 %collective-permute-start.5 = (f32[15,64,128]{2,1,0:T(8,128)S(1)}, f32[15,64,128]{2,1,0:T(8,128)S(1)}, u32[]{:S(2)}, u32[]{:S(2)}) collective-permute-start(f32[15,64,128]{2,1,0:T(8,128)S(1)} %get-tuple-element.8), channel_id=1, source_target_pairs={{1,0},{2,1},{3,2},{4,3},{5,4},{6,5},{7,6},{8,7},{9,8},{10,9},{11,1... | collective-permute-start | bytes 1474568 | tf_op jit(solution)/shard_map/ppermute | solution.py:20
  226.9 0.6 copy.86
  227.5 3.9 %collective-permute-done.4 = f32[15,64,128]{2,1,0:T(8,128)S(1)} collective-permute-done((f32[15,64,128]{2,1,0:T(8,128)S(1)}, f32[15,64,128]{2,1,0:T(8,128)S(1)}, u32[]{:S(2)}, u32[]{:S(2)}) %collective-permute-start.4) | collective-permute-done | bytes 491552 | tf_op jit(solution)/shard_map/ppermute | solution.py:17
  231.5 0.3 copy.55
  231.8 1.3 collective-permute-done.5
  233.1 0.3 copy.57
  233.4 0.2 pad_maximum_fusion.1
  233.6 0.4 copy.58
  234.0 0.2 slice_bitcast_fusion.1
  234.2 2.3 fusion.2
  236.5 1.6 convolution_bitcast_fusion.1
  238.1 1.0 fusion.14
  239.2 5.8 %collective-permute-start.6 = (f32[15,64,128]{2,1,0:T(8,128)S(1)}, f32[15,64,128]{2,1,0:T(8,128)S(1)}, u32[]{:S(2)}, u32[]{:S(2)}) collective-permute-start(f32[15,64,128]{2,1,0:T(8,128)S(1)} %get-tuple-element.5), channel_id=1, source_target_pairs={{0,1},{1,2},{2,3},{3,4},{4,5},{5,6},{6,7},{7,8},{8,9},{9,10},{10,1... | collective-permute-start | bytes 1474568 | tf_op jit(solution)/shard_map/ppermute | solution.py:17
  245.0 3.0 collective-permute-start.7
  248.0 4.4 %collective-permute-done.6 = f32[15,64,128]{2,1,0:T(8,128)S(1)} collective-permute-done((f32[15,64,128]{2,1,0:T(8,128)S(1)}, f32[15,64,128]{2,1,0:T(8,128)S(1)}, u32[]{:S(2)}, u32[]{:S(2)}) %collective-permute-start.6) | collective-permute-done | bytes 491552 | tf_op jit(solution)/shard_map/ppermute | solution.py:17
  252.4 1.7 collective-permute-done.7
  254.1 0.2 pad_maximum_fusion.3
  254.4 0.2 slice_bitcast_fusion
  254.6 2.3 fusion
  256.9 1.6 convolution_bitcast_fusion
  258.5 1.9 fusion.70
  260.5 93.0 %reduce-scatter.5.cloned.1.call-done = f32[32,8,128]{2,1,0:T(8,128)} async-done(((f32[32,64,128]{2,1,0:T(8,128)}), f32[32,8,128]{2,1,0:T(8,128)}) %reduce-scatter.5.cloned.1.call-update) | async-done | bytes 131088 | tf_op jit(solution)/shard_map/reduce_scatter | solution.py:105
  353.5 1.6 bitcast_divide_fusion
  (46 shorter events, 2.4 us)
Async XLA Ops:
  6.5 14.8 %copy-start.1 = (f32[8,3,31]{2,0,1:T(8,128)S(1)}, f32[8,3,31]{2,0,1:T(8,128)}, u32[]{:S(2)}) copy-start(f32[8,3,31]{2,0,1:T(8,128)} %param.6) | copy-start | bytes 8932
  6.5 15.1 %copy-start.4 = (s32[8,16]{1,0:T(8,128)S(1)}, s32[8,16]{1,0:T(8,128)}, u32[]{:S(2)}) copy-start(s32[8,16]{1,0:T(8,128)} %param.7) | copy-start | bytes 1540
  8.5 41.5 %all-to-all-start = ((f32[8,32,8,128]{3,2,1,0:T(8,128)}), f32[8,32,8,128]{3,2,1,0:T(8,128)S(1)}, u32[]{:S(2)}, u32[]{:S(2)}) async-start(f32[8,32,8,128]{3,2,1,0:T(8,128)} %stack.4), calls=%async_computation | async-start | bytes 2097152 | tf_op jit(solution)/shard_map/all_to_all | solution.py:98
  21.3 165.9 %reduce-scatter.3.cloned.1.call-start = ((), (), s32[]{:S(2)}) async-start(), calls=%async_computation.4 | async-start | bytes 1179648 | tf_op jit(solution)/shard_map/reduce_scatter | solution.py:105
  50.2 13.0 %collective-permute-start = (f32[15,64,128]{2,1,0:T(8,128)S(1)}, f32[15,64,128]{2,1,0:T(8,128)S(1)}, u32[]{:S(2)}, u32[]{:S(2)}) collective-permute-start(f32[15,64,128]{2,1,0:T(8,128)S(1)} %get-tuple-element.13), channel_id=1, source_target_pairs={{0,1},{1,2},{2,3},{3,4},{4,5},{5,6},{6,7},{7,8},{8,9},{9,10},{10,1... | collective-permute-start | bytes 1474568 | tf_op jit(solution)/shard_map/ppermute | solution.py:17
  52.1 12.7 %collective-permute-start.1 = (f32[15,64,128]{2,1,0:T(8,128)S(1)}, f32[15,64,128]{2,1,0:T(8,128)S(1)}, u32[]{:S(2)}, u32[]{:S(2)}) collective-permute-start(f32[15,64,128]{2,1,0:T(8,128)S(1)} %get-tuple-element.14), channel_id=1, source_target_pairs={{1,0},{2,1},{3,2},{4,3},{5,4},{6,5},{7,6},{8,7},{9,8},{10,9},{11,1... | collective-permute-start | bytes 1474568 | tf_op jit(solution)/shard_map/ppermute | solution.py:20
  66.0 3.9 %copy-start.2 = (f32[1,32,64,128]{3,2,1,0:T(8,128)S(1)}, f32[1,32,64,128]{3,2,1,0:T(8,128)}, u32[]{:S(2)}) copy-start(f32[1,32,64,128]{3,2,1,0:T(8,128)} %param.5) | copy-start | bytes 3145732
  71.0 13.2 %collective-permute-start.2 = (f32[15,64,128]{2,1,0:T(8,128)S(1)}, f32[15,64,128]{2,1,0:T(8,128)S(1)}, u32[]{:S(2)}, u32[]{:S(2)}) collective-permute-start(f32[15,64,128]{2,1,0:T(8,128)S(1)} %get-tuple-element.11), channel_id=1, source_target_pairs={{0,1},{1,2},{2,3},{3,4},{4,5},{5,6},{6,7},{7,8},{8,9},{9,10},{10,1... | collective-permute-start | bytes 1474568 | tf_op jit(solution)/shard_map/ppermute | solution.py:17
  76.3 9.5 %collective-permute-start.3 = (f32[15,64,128]{2,1,0:T(8,128)S(1)}, f32[15,64,128]{2,1,0:T(8,128)S(1)}, u32[]{:S(2)}, u32[]{:S(2)}) collective-permute-start(f32[15,64,128]{2,1,0:T(8,128)S(1)} %get-tuple-element.12), channel_id=1, source_target_pairs={{1,0},{2,1},{3,2},{4,3},{5,4},{6,5},{7,6},{8,7},{9,8},{10,9},{11,1... | collective-permute-start | bytes 1474568 | tf_op jit(solution)/shard_map/ppermute | solution.py:20
  92.0 95.1 %copy-start = (f32[32,8,128]{2,1,0:T(8,128)S(1)}, f32[32,8,128]{2,1,0:T(8,128)}, u32[]{:S(2)}) copy-start(f32[32,8,128]{2,1,0:T(8,128)} %param.4) | copy-start | bytes 393220
  92.1 261.5 %reduce-scatter.5.cloned.1.call-start = ((), (), s32[]{:S(2)}) async-start(), calls=%async_computation.5 | async-start | bytes 1179648 | tf_op jit(solution)/shard_map/reduce_scatter | solution.py:105
  218.4 13.0 %collective-permute-start.4 = (f32[15,64,128]{2,1,0:T(8,128)S(1)}, f32[15,64,128]{2,1,0:T(8,128)S(1)}, u32[]{:S(2)}, u32[]{:S(2)}) collective-permute-start(f32[15,64,128]{2,1,0:T(8,128)S(1)} %get-tuple-element.7), channel_id=1, source_target_pairs={{0,1},{1,2},{2,3},{3,4},{4,5},{5,6},{6,7},{7,8},{8,9},{9,10},{10,1... | collective-permute-start | bytes 1474568 | tf_op jit(solution)/shard_map/ppermute | solution.py:17
  220.3 12.7 %collective-permute-start.5 = (f32[15,64,128]{2,1,0:T(8,128)S(1)}, f32[15,64,128]{2,1,0:T(8,128)S(1)}, u32[]{:S(2)}, u32[]{:S(2)}) collective-permute-start(f32[15,64,128]{2,1,0:T(8,128)S(1)} %get-tuple-element.8), channel_id=1, source_target_pairs={{1,0},{2,1},{3,2},{4,3},{5,4},{6,5},{7,6},{8,7},{9,8},{10,9},{11,1... | collective-permute-start | bytes 1474568 | tf_op jit(solution)/shard_map/ppermute | solution.py:20
  234.2 3.9 %copy-start.3 = (f32[1,32,64,128]{3,2,1,0:T(8,128)S(1)}, f32[1,32,64,128]{3,2,1,0:T(8,128)}, u32[]{:S(2)}) copy-start(f32[1,32,64,128]{3,2,1,0:T(8,128)} %param.5) | copy-start | bytes 3145732
  239.2 13.2 %collective-permute-start.6 = (f32[15,64,128]{2,1,0:T(8,128)S(1)}, f32[15,64,128]{2,1,0:T(8,128)S(1)}, u32[]{:S(2)}, u32[]{:S(2)}) collective-permute-start(f32[15,64,128]{2,1,0:T(8,128)S(1)} %get-tuple-element.5), channel_id=1, source_target_pairs={{0,1},{1,2},{2,3},{3,4},{4,5},{5,6},{6,7},{7,8},{8,9},{9,10},{10,1... | collective-permute-start | bytes 1474568 | tf_op jit(solution)/shard_map/ppermute | solution.py:17
  245.0 9.1 %collective-permute-start.7 = (f32[15,64,128]{2,1,0:T(8,128)S(1)}, f32[15,64,128]{2,1,0:T(8,128)S(1)}, u32[]{:S(2)}, u32[]{:S(2)}) collective-permute-start(f32[15,64,128]{2,1,0:T(8,128)S(1)} %get-tuple-element.6), channel_id=1, source_target_pairs={{1,0},{2,1},{3,2},{4,3},{5,4},{6,5},{7,6},{8,7},{9,8},{10,9},{11,1... | collective-permute-start | bytes 1474568 | tf_op jit(solution)/shard_map/ppermute | solution.py:20
Sparse Core Ops, SparseCore 0:
  92.2 94.8 reduce-scatter.2
  260.6 92.8 reduce-scatter.4
